TPU v7x, 32 devices: a whole 2x2x4 slice. The times are simulated.
32 devices in a mesh: domain: 2 (over core), shard: 16 (over z, y, x).
Axes of the slice: x: 2, y: 2, z: 4, core: 2. Of those that a mesh axis runs over, the one named last changes fastest.
Arguments:
- gradients: bfloat16 [2, 128, 4096], P('domain', 'shard'), may hold values from -64 to 64
- pair_blocks: int32 [2, 2], replicated, may hold values from 0 to 4, as said below
Outputs:
- influence: float32 [2, 128, 48], P('domain', 'shard')
Inputs may be any that keep to these rules, and one draw needn't show every extreme that they name: pair_blocks is symmetric; some pair takes 4 blocks in every draw.
All inputs are finite; a program needn't handle non-finite values.
Results may differ from a plain program's by a relative error of at most 0.00039.
Values may be sent and summed in bfloat16 or wider, within the bound.
A program may use at most 64 MiB of HBM per device.

v0:
```python
import math

import jax
import jax.numpy as jnp
from jax import lax
from jax.sharding import PartitionSpec as P

BLOCK_WIDTH = 64
COUNT_MAX = 4


damping = 0.5


def shifted(value, axis, steps):
    count = lax.axis_size(axis)
    pairs = [(source, (source + steps) % count) for source in range(count)]
    return lax.ppermute(value, axis, pairs)


def invert(statistics, example_total):
    traces = jnp.einsum("bpp->b", statistics)
    order = statistics.shape[-1]
    identity = jnp.eye(order, dtype=jnp.float32)
    fisher = (
        statistics / example_total
        + (damping * traces / (order * example_total))[:, None, None] * identity
    )
    factor = jnp.linalg.cholesky(fisher)
    identities = jnp.broadcast_to(identity, fisher.shape)
    factor_inv = lax.linalg.triangular_solve(factor, identities, left_side=True, lower=True)
    return jnp.einsum("bkp,bkq->bpq", factor_inv, factor_inv, precision=lax.Precision.HIGHEST)


def local(gradients, pair_blocks):
    own_rows = gradients[0]
    examples_here, full_width = own_rows.shape
    module_count = full_width // BLOCK_WIDTH
    domain_count = lax.axis_size("domain")
    example_total = examples_here * domain_count * lax.axis_size("shard")
    blocked = own_rows.reshape(examples_here, module_count, BLOCK_WIDTH)
    statistics = jnp.einsum("ibp,ibq->bpq", blocked, blocked, preferred_element_type=jnp.float32)
    partial_sum = lax.psum_scatter(statistics, "shard", scatter_dimension=0, tiled=True)
    partial_sum = lax.psum(partial_sum, "domain")
    inverse = lax.all_gather(invert(partial_sum, example_total), "shard", axis=0, tiled=True)
    precond = jnp.einsum(
        "ibp,bpq->ibq", blocked.astype(jnp.float32), inverse, precision=lax.Precision.HIGHEST
    )
    precond = precond.reshape(examples_here, full_width).astype(jnp.bfloat16)
    inv_root = 1.0 / math.sqrt(full_width)
    domain_index = lax.axis_index("domain")
    row_pieces = []
    for step_by in (-1, 0, 1):
        if step_by == 0:
            row_pieces.append(precond)
        else:
            row_pieces.append(shifted(precond, "shard", step_by))
    queries = jnp.concatenate(row_pieces, 0)
    wide = domain_count * examples_here
    direct = (
        jnp.einsum(
            "ik,jk->ij",
            queries,
            lax.all_gather(own_rows, "domain", axis=0, tiled=True),
            preferred_element_type=jnp.float32,
        )
        * inv_root
    )
    row_blocks = direct.reshape(3, examples_here, wide)
    received = []
    for step_by in (-1, 0, 1):
        if step_by == 0:
            received.append(row_blocks[1])
        else:
            received.append(shifted(row_blocks[step_by + 1], "shard", -step_by))
    final = jnp.stack(received, 0)
    raw_tiles = jnp.transpose(final, (1, 0, 2)).reshape(examples_here, 3 * wide)
    counts = lax.dynamic_index_in_dim(pair_blocks, domain_index, 0, keepdims=False)
    column_all = jnp.arange(3 * wide, dtype=jnp.int32)
    column_domain = column_all // examples_here % domain_count
    limits = jnp.take(counts * (examples_here // COUNT_MAX), column_domain)
    column_index = column_all % examples_here
    row_index = jnp.arange(examples_here, dtype=jnp.int32)
    kept_mask = (row_index[:, None] < limits[None, :]) & (column_index < limits)[None, :]
    return jnp.where(kept_mask, raw_tiles, 0.0)[None]


def solution(mesh):
    placed = (P("domain", "shard", None), P())
    return jax.shard_map(
        local, mesh=mesh, in_specs=placed, out_specs=P("domain", "shard", None), check_vma=False
    )
```

profile of v0, /device:TPU:0, one launch (start us, length us, event | category | flops | bytes accessed | tf_op | source)
XLA Modules:
  0.0 249.4 jit_solution(4142268824427378098)
XLA Ops:
  6.5 0.0 reduce-scatter.2.cloned.1.call-start
  6.5 1.0 reshape_squeeze.3
  7.6 1.8 fusion.11
  9.4 0.0 copy-start.1
  9.4 0.0 reduce-scatter.2.cloned.1.call-update
  9.4 0.0 all-reduce.2.cloned.1.call-start
  9.5 84.3 %reduce-scatter.2.cloned.1.call-done = f32[4,64,64]{2,1,0:T(8,128)} async-done(((f32[64,64,64]{2,1,0:T(8,128)}), f32[4,64,64]{2,1,0:T(8,128)}) %reduce-scatter.2.cloned.1.call-update) | async-done | bytes 65552 | tf_op jit(solution)/shard_map/reduce_scatter | solution.py:43
  93.8 0.0 all-reduce.2.cloned.1.call-update
  93.8 0.0 all-gather.3.cloned.1.call-start
  93.9 16.8 %all-reduce.2.cloned.1.call-done = f32[4,64,64]{2,1,0:T(8,128)} async-done(((f32[4,64,64]{2,1,0:T(8,128)}), f32[4,64,64]{2,1,0:T(8,128)}) %all-reduce.2.cloned.1.call-update) | async-done | bytes 65552 | tf_op jit(solution)/shard_map/psum | solution.py:44
  110.7 1.0 select_reduce_fusion.1
  111.8 1.0 multiply_add_fusion
  112.7 0.1 copy.32
  112.9 1.0 fusion.9
  113.8 0.0 copy-start
  113.9 23.5 %custom-call.7 = f32[4,64,64]{2,1,0:T(8,128)S(1)} custom-call(f32[4,64,64]{2,1,0:T(8,128)S(1)} %fusion.9), custom_call_target="Cholesky" | custom-call | tf_op jit(solution)/shard_map/jit(cholesky)/cholesky | solution.py:29
  137.4 0.1 compare_reduce_fusion
  137.5 0.1 select_bitcast_fusion
  137.6 19.7 %custom-call.8 = f32[4,1,64,64]{2,3,1,0:T(8,128)S(1)} custom-call(f32[4,1,64,64]{3,2,1,0:T(8,128)S(1)} %select_bitcast_fusion), custom_call_target="InvertDiagBlocksLowerTriangular" | custom-call | tf_op jit(solution)/shard_map/triangular_solve | solution.py:31
  157.2 0.4 fusion.7
  157.6 1.0 fusion.24
  158.7 0.0 all-gather.3.cloned.1.call-update
  158.7 0.0 copy-done.1
  158.7 61.7 %all-gather.3.cloned.1.call-done = f32[64,64,64]{2,1,0:T(8,128)} async-done(((f32[4,64,64]{2,1,0:T(8,128)}), f32[64,64,64]{2,1,0:T(8,128)}) %all-gather.3.cloned.1.call-update) | async-done | bytes 1048592 | tf_op jit(solution)/shard_map/all_gather | solution.py:45
  220.4 2.7 %fusion = bf16[8,64,64]{2,0,1:T(8,128)(2,1)S(1)} fusion(f32[64,64,64]{2,1,0:T(8,128)} %all-gather.3.cloned.1.call-done, bf16[8,64,64]{2,1,0:T(8,128)(2,1)S(1)} %reshape_squeeze.3), kind=kOutput, calls=%fused_computation.1 | convolution fusion | flops 25198592 | bytes 1179648 | tf_op jit(solution)/shard_map/ibp,bpq->ibq/dot_general | solution.py:46
  223.2 0.2 convert_element_type.22
  223.4 3.1 %collective-permute-start = (bf16[8,4096]{1,0:T(8,128)(2,1)S(1)}, bf16[8,4096]{1,0:T(8,128)(2,1)S(1)}, u32[]{:S(2)}, u32[]{:S(2)}) collective-permute-start(bf16[8,4096]{1,0:T(8,128)(2,1)S(1)} %convert_element_type.22), channel_id=1, source_target_pairs={{0,15},{1,0},{2,1},{3,2},{4,3},{5,4},{6,5},{7,6},{8,7},{9,8},{10,9... | collective-permute-start | bytes 196616 | tf_op jit(solution)/shard_map/ppermute | solution.py:18
  226.4 0.0 collective-permute-start.1
  226.4 0.6 fusion.23
  227.0 0.0 copy-done
  227.0 1.9 all-gather
  228.9 0.0 collective-permute-done
  228.9 5.4 %collective-permute-done.1 = bf16[8,4096]{1,0:T(8,128)(2,1)S(1)} collective-permute-done((bf16[8,4096]{1,0:T(8,128)(2,1)S(1)}, bf16[8,4096]{1,0:T(8,128)(2,1)S(1)}, u32[]{:S(2)}, u32[]{:S(2)}) %collective-permute-start.1) | collective-permute-done | bytes 65568 | tf_op jit(solution)/shard_map/ppermute | solution.py:18
  234.3 0.2 convolution_multiply_fusion
  234.5 0.1 fusion.22
  234.6 0.3 collective-permute-start.3
  234.8 1.8 collective-permute-start.2
  236.6 1.3 fusion.17
  237.9 0.1 copy.38
  237.9 0.3 collective-permute-done.3
  238.2 0.1 copy.39
  238.3 3.8 %collective-permute-done.2 = f32[8,16]{0,1:T(8,128)S(1)} collective-permute-done((f32[8,16]{0,1:T(8,128)S(1)}, f32[8,16]{0,1:T(8,128)S(1)}, u32[]{:S(2)}, u32[]{:S(2)}) %collective-permute-start.2) | collective-permute-done | bytes 544 | tf_op jit(solution)/shard_map/ppermute | solution.py:18
  242.1 0.1 copy.37
  242.2 0.1 reshape.225
  242.2 0.6 fusion.16
  (10 shorter events, 0.1 us)
Async XLA Ops:
  6.5 87.3 %reduce-scatter.2.cloned.1.call-start = ((), (), s32[]{:S(2)}) async-start(), calls=%async_computation.1 | async-start | bytes 2228224 | tf_op jit(solution)/shard_map/reduce_scatter | solution.py:43
  9.4 149.3 %copy-start.1 = (s32[2,2]{1,0:T(2,128)S(1)}, s32[2,2]{1,0:T(2,128)}, u32[]{:S(2)}) copy-start(s32[2,2]{1,0:T(2,128)} %param.3) | copy-start | bytes 52
  9.4 101.3 %all-reduce.2.cloned.1.call-start = ((), (), s32[]{:S(2)}) async-start(), calls=%async_computation.2 | async-start | bytes 262144 | tf_op jit(solution)/shard_map/psum | solution.py:44
  93.8 126.6 %all-gather.3.cloned.1.call-start = ((), (), s32[]{:S(2)}) async-start(), calls=%async_computation.3 | async-start | bytes 2228224 | tf_op jit(solution)/shard_map/all_gather | solution.py:45
  113.8 113.2 %copy-start = (bf16[1,8,4096]{2,1,0:T(8,128)(2,1)S(1)}, bf16[1,8,4096]{2,1,0:T(8,128)(2,1)}, u32[]{:S(2)}) copy-start(bf16[1,8,4096]{2,1,0:T(8,128)(2,1)} %param.2) | copy-start | bytes 196612
  223.4 5.6 %collective-permute-start = (bf16[8,4096]{1,0:T(8,128)(2,1)S(1)}, bf16[8,4096]{1,0:T(8,128)(2,1)S(1)}, u32[]{:S(2)}, u32[]{:S(2)}) collective-permute-start(bf16[8,4096]{1,0:T(8,128)(2,1)S(1)} %convert_element_type.22), channel_id=1, source_target_pairs={{0,15},{1,0},{2,1},{3,2},{4,3},{5,4},{6,5},{7,6},{8,7},{9,8},{10,9... | collective-permute-start | bytes 196616 | tf_op jit(solution)/shard_map/ppermute | solution.py:18
  226.4 7.9 %collective-permute-start.1 = (bf16[8,4096]{1,0:T(8,128)(2,1)S(1)}, bf16[8,4096]{1,0:T(8,128)(2,1)S(1)}, u32[]{:S(2)}, u32[]{:S(2)}) collective-permute-start(bf16[8,4096]{1,0:T(8,128)(2,1)S(1)} %convert_element_type.22), channel_id=1, source_target_pairs={{0,1},{1,2},{2,3},{3,4},{4,5},{5,6},{6,7},{7,8},{8,9},{9,10},{10,1... | collective-permute-start | bytes 196616 | tf_op jit(solution)/shard_map/ppermute | solution.py:18
  234.6 3.7 %collective-permute-start.3 = (f32[8,16]{0,1:T(8,128)S(1)}, f32[8,16]{0,1:T(8,128)S(1)}, u32[]{:S(2)}, u32[]{:S(2)}) collective-permute-start(f32[8,16]{0,1:T(8,128)S(1)} %get-tuple-element.8), channel_id=1, source_target_pairs={{0,15},{1,0},{2,1},{3,2},{4,3},{5,4},{6,5},{7,6},{8,7},{9,8},{10,9... | collective-permute-start | bytes 1544 | tf_op jit(solution)/shard_map/ppermute | solution.py:18
  234.8 7.2 %collective-permute-start.2 = (f32[8,16]{0,1:T(8,128)S(1)}, f32[8,16]{0,1:T(8,128)S(1)}, u32[]{:S(2)}, u32[]{:S(2)}) collective-permute-start(f32[8,16]{0,1:T(8,128)S(1)} %get-tuple-element.7), channel_id=1, source_target_pairs={{0,1},{1,2},{2,3},{3,4},{4,5},{5,6},{6,7},{7,8},{8,9},{9,10},{10,1... | collective-permute-start | bytes 1544 | tf_op jit(solution)/shard_map/ppermute | solution.py:18
Sparse Core Ops, SparseCore 0:
  9.6 84.1 reduce-scatter.1
  96.1 14.5 all-reduce.1
  158.8 61.5 all-gather.2
where the time goes:
time: 250 us; the launch traced here: 249 us
  waiting for transfers between devices  172 us (69%)
  other arithmetic  48.3 us (19%)
  between operations  13.2 us (5%)
  matrix products  6.15 us (2%)
  starting transfers between devices  5.21 us (2%)
    reduce_scatter x1, waiting for transfers between devices, local(): lax.psum_scatter(statistics, 'shard', scatter_dimension=0, tiled=True)  84.3 us
    all_gather x1, waiting for transfers between devices, local(): lax.all_gather(invert(partial_sum, example_total), 'shard', axis=0, tiled...  61.7 us
    another operation x4, other arithmetic, invert(): factor = jnp.linalg.cholesky(fisher)  23.6 us
    another operation x3, other arithmetic, invert(): lax.linalg.triangular_solve(factor, identities, left_side=True, lower=True)  19.8 us
    psum x1, waiting for transfers between devices, local(): partial_sum = lax.psum(partial_sum, 'domain')  16.8 us
    ppermute x4, waiting for transfers between devices, shifted(): return lax.ppermute(value, axis, pairs)  9.43 us
    ppermute x4, starting transfers between devices, shifted(): return lax.ppermute(value, axis, pairs)  5.12 us
  transfers between devices with their start and end apart: 7, of which 6 were waited for; matrix products, arithmetic and copies ran while one was open for 1% of the time, Pallas kernels for 0%

commit v1 on v0

--- a/solution.py
+++ b/solution.py
@@ -1,15 +1,191 @@
+import functools
 import math
 
 import jax
 import jax.numpy as jnp
 from jax import lax
+from jax.experimental import pallas as pl
+from jax.experimental.pallas import tpu as pltpu
 from jax.sharding import PartitionSpec as P
 
 BLOCK_WIDTH = 64
 COUNT_MAX = 4
+LANES = 128
+STEPS = (-1, 0, 1)
 
 
 damping = 0.5
+
+
+def split(value):
+    high = value.astype(jnp.bfloat16)
+    rest = value - high.astype(jnp.float32)
+    middle = rest.astype(jnp.bfloat16)
+    low = (rest - middle.astype(jnp.float32)).astype(jnp.bfloat16)
+    return high, middle, low
+
+
+def exact_dot(left, right):
+    return jnp.dot(
+        left, right, preferred_element_type=jnp.float32, precision=lax.Precision.HIGHEST
+    )
+
+
+def invert_modules(statistics, example_total):
+    order = BLOCK_WIDTH
+    width = statistics.shape[0]
+    row = lax.broadcasted_iota(jnp.int32, (width, width), 0)
+    column = lax.broadcasted_iota(jnp.int32, (width, width), 1)
+    same = row // order == column // order
+    diagonal = row == column
+    identity = jnp.where(diagonal, 1.0, 0.0)
+    entries = jnp.sum(jnp.where(diagonal, statistics, 0.0), axis=0, keepdims=True)
+    lane = lax.broadcasted_iota(jnp.int32, (1, width), 1) // order
+    traces = jnp.zeros((1, width), jnp.float32)
+    for module in range(width // order):
+        here = lane == module
+        total = jnp.sum(jnp.where(here, entries, 0.0), axis=1, keepdims=True)
+        traces = jnp.where(here, total, traces)
+    scale = order / traces
+    scaled = jnp.where(same, statistics * scale, 0.0) + damping * identity
+    low, high = damping, order + damping
+    bound = (high + low) / (high - low)
+    residual = identity - (2.0 / (high + low)) * scaled
+    now, later = bound, 2.0 * bound * bound - 1.0
+    gain = 2.0 * now * now / later
+    inverse = (gain * 2.0 / (high + low)) * (identity + residual)
+    residual = gain * exact_dot(residual, residual) - (1.0 / later) * identity
+    while later < 1e4:
+        now, later = later, 2.0 * later * later - 1.0
+        gain = 2.0 * now * now / later
+        both = exact_dot(jnp.concatenate([inverse, residual], 0), residual)
+        inverse = gain * (inverse + both[:width])
+        residual = gain * both[width:] - (1.0 / later) * identity
+    error = identity - exact_dot(scaled, inverse)
+    inverse = inverse + exact_dot(inverse, error)
+    return inverse * (scale * example_total)
+
+
+def kernel(domain_count, shard_count, grads, pairs, out, own, rows_in, tiles_out, tiles_in,
+           load_sem, send_sem, recv_sem, send_sem2, recv_sem2):
+    devices = domain_count * shard_count
+    domain, shard = lax.axis_index("domain"), lax.axis_index("shard")
+    here = shard * domain_count + domain
+    examples, full_width = own.shape
+    width = full_width // devices
+    wide = domain_count * examples
+    total = devices * examples
+
+    def place(index):
+        return {"domain": lax.rem(index, domain_count), "shard": lax.div(index, domain_count)}
+
+    load = pltpu.make_async_copy(grads, own, load_sem)
+    load.start()
+    others = [lax.rem(here + step, devices) for step in range(1, devices)]
+    barrier = pltpu.get_barrier_semaphore()
+    for other in others:
+        pl.semaphore_signal(
+            barrier, inc=1, device_id=place(other), device_id_type=pl.DeviceIdType.MESH
+        )
+    load.wait()
+    mine = pl.ds(pl.multiple_of(here * width, LANES), width)
+    rows_in[pl.ds(here, 1)] = own[:, mine][None]
+    pl.semaphore_wait(barrier, devices - 1)
+
+    first = []
+    for step, other in enumerate(others):
+        copy = pltpu.make_async_remote_copy(
+            src_ref=own.at[:, pl.ds(pl.multiple_of(other * width, LANES), width)],
+            dst_ref=rows_in.at[here],
+            send_sem=send_sem.at[step],
+            recv_sem=recv_sem.at[step],
+            device_id=place(other),
+            device_id_type=pl.DeviceIdType.MESH,
+        )
+        copy.start()
+        first.append(copy)
+    for copy in first:
+        copy.wait()
+
+    rows = rows_in[...].astype(jnp.float32).reshape(total, width).astype(jnp.bfloat16)
+    statistics = lax.dot_general(
+        rows, rows, (((0,), (0,)), ((), ())), preferred_element_type=jnp.float32
+    )
+    inverse = invert_modules(statistics, float(total))
+    precond = jnp.zeros((total, width), jnp.float32)
+    for term in split(inverse)[::-1]:
+        precond = precond + jnp.dot(rows, term, preferred_element_type=jnp.float32)
+    products = lax.dot_general(
+        precond.astype(jnp.bfloat16), rows, (((1,), (1,)), ((), ())),
+        preferred_element_type=jnp.float32,
+    )
+    taken = tiles_out.shape[-1]
+    for position in range(shard_count):
+        band = products[position * wide:(position + 1) * wide]
+        start = (position + STEPS[0]) * wide % total
+        band = pltpu.roll(band, (total - start) % total, 1)[:, :taken]
+        for number in range(domain_count):
+            tiles_out[position * domain_count + number] = band[
+                number * examples:(number + 1) * examples
+            ]
+    tiles_in[pl.ds(here, 1)] = tiles_out[pl.ds(here, 1)]
+
+    second = []
+    for step, other in enumerate(others):
+        copy = pltpu.make_async_remote_copy(
+            src_ref=tiles_out.at[other],
+            dst_ref=tiles_in.at[here],
+            send_sem=send_sem2.at[step],
+            recv_sem=recv_sem2.at[step],
+            device_id=place(other),
+            device_id_type=pl.DeviceIdType.MESH,
+        )
+        copy.start()
+        second.append(copy)
+
+    column = lax.broadcasted_iota(jnp.int32, (examples, taken), 1)
+    column_domain = lax.rem(lax.div(column, examples), domain_count)
+    limits = jnp.zeros((examples, taken), jnp.int32)
+    for number in range(domain_count):
+        limit = pairs[domain, number] * (examples // COUNT_MAX)
+        limits = jnp.where(column_domain == number, limit, limits)
+    row = lax.broadcasted_iota(jnp.int32, (examples, taken), 0)
+    kept = (row < limits) & (lax.rem(column, examples) < limits)
+    for copy in second:
+        copy.wait()
+    influence = jnp.sum(tiles_in[...], axis=0) * (1.0 / math.sqrt(full_width))
+    influence = jnp.where(kept, influence, 0.0)
+    out[...] = influence[:, :out.shape[-1]]
+
+
+def fused(gradients, pair_blocks):
+    domain_count, shard_count = lax.axis_size("domain"), lax.axis_size("shard")
+    devices = domain_count * shard_count
+    examples, full_width = gradients.shape[1:]
+    width = full_width // devices
+    columns = len(STEPS) * domain_count * examples
+    taken = pl.cdiv(columns, LANES) * LANES
+    dma = pltpu.SemaphoreType.DMA((devices - 1,))
+    result = pl.pallas_call(
+        functools.partial(kernel, domain_count, shard_count),
+        out_shape=jax.ShapeDtypeStruct((examples, columns), jnp.float32),
+        in_specs=[
+            pl.BlockSpec(memory_space=pl.ANY),
+            pl.BlockSpec(memory_space=pltpu.SMEM),
+        ],
+        out_specs=pl.BlockSpec(memory_space=pltpu.VMEM),
+        scratch_shapes=[
+            pltpu.VMEM((examples, full_width), gradients.dtype),
+            pltpu.VMEM((devices, examples, width), gradients.dtype),
+            pltpu.VMEM((devices, examples, taken), jnp.float32),
+            pltpu.VMEM((devices, examples, taken), jnp.float32),
+            pltpu.SemaphoreType.DMA,
+            dma, dma, dma, dma,
+        ],
+        compiler_params=pltpu.CompilerParams(collective_id=0, has_side_effects=True),
+        name="influence",
+    )(gradients[0], pair_blocks)
+    return result[None]
 
 
 def shifted(value, axis, steps):
@@ -87,6 +263,17 @@
 
 def solution(mesh):
     placed = (P("domain", "shard", None), P())
+
+    def body(gradients, pair_blocks):
+        domain_count, shard_count = mesh.shape["domain"], mesh.shape["shard"]
+        devices = domain_count * shard_count
+        examples, full_width = gradients.shape[1:]
+        columns = len(STEPS) * domain_count * examples
+        whole_modules = full_width % (devices * math.lcm(LANES, BLOCK_WIDTH)) == 0
+        if whole_modules and examples % 8 == 0 and columns <= devices * examples:
+            return fused(gradients, pair_blocks)
+        return local(gradients, pair_blocks)
+
     return jax.shard_map(
-        local, mesh=mesh, in_specs=placed, out_specs=P("domain", "shard", None), check_vma=False
-    )
+        body, mesh=mesh, in_specs=placed, out_specs=P("domain", "shard", None), check_vma=False
+    )

time: 250 us -> 23.5 us (0.09)
  waiting for transfers between devices: 172 us -> 0 us
  other arithmetic: 48.3 us -> 0 us
  Pallas kernels: 0 us -> 22 us
  between operations: 13.2 us -> 0.01 us
  matrix products: 6.15 us -> 0 us
  starting transfers between devices: 5.21 us -> 0 us
    reduce_scatter x1 -> x0, waiting for transfers between devices: 84.3 us -> none  [local(): lax.psum_scatter(statistics, 'shard', scatter_dimension=0, tiled=True)]
    all_gather x1 -> x0, waiting for transfers between devices: 61.7 us -> none  [local(): lax.all_gather(invert(partial_sum, example_total), 'shard', axis=0, tiled...]
    another operation x7 -> x0, other arithmetic: 43.4 us -> none  [the longest x4 23.6 us: invert(): factor = jnp.linalg.cholesky(fisher)]
    pallas_call x0 -> x1, Pallas kernels: none -> 22 us  [fused(): pl.pallas_call(functools.partial(kernel, domain_count, shard_count), out_...]
    psum x1 -> x0, waiting for transfers between devices: 16.8 us -> none  [local(): partial_sum = lax.psum(partial_sum, 'domain')]
    ppermute x4 -> x0, waiting for transfers between devices: 9.43 us -> none  [shifted(): return lax.ppermute(value, axis, pairs)]
    dot_general x4 -> x0, matrix products: 5.74 us -> none  [the longest x1 2.7 us: local(): jnp.einsum('ibp,bpq->ibq', blocked.astype(jnp.float32), inverse, precisio...]
    ppermute x4 -> x0, starting transfers between devices: 5.12 us -> none  [shifted(): return lax.ppermute(value, axis, pairs)]
  transfers between devices with their start and end apart: 7 -> 0, of which waited for: 6 -> 0; matrix products, arithmetic and copies ran while one was open for 1% -> 0% of each run, Pallas kernels for 0% -> 0%
where the time goes in v1:
time: 23.5 us; the launch traced here: 23.3 us
  Pallas kernels  22 us (94%)
  local copies, waits for them, and re-layouts  1.28 us (5%)
    pallas_call x1, Pallas kernels, fused(): pl.pallas_call(functools.partial(kernel, domain_count, shard_count), out_...  22 us
    unnamed x1, local copies, waits for them, and re-layouts  1.28 us

profile of v1, /device:TPU:0, one launch (start us, length us, event | category | flops | bytes accessed | tf_op | source)
XLA Modules:
  0.0 23.3 jit_solution(8999347066023710434)
XLA Ops:
  0.0 22.0 %influence.1 = f32[8,48]{1,0:T(8,128)} custom-call(bf16[8,4096]{1,0:T(8,128)(2,1)} %bitcast.2, s32[2,2]{1,0:T(2,128)} %pairs.1), custom_call_target="tpu_custom_call" | custom-call | tf_op jit(solution)/shard_map/influence/pallas_call | solution.py:169
  22.0 1.3 %copy.4 = f32[1,8,48]{2,1,0:T(8,128)} copy(f32[1,8,48]{2,1,0:T(8,128)} %bitcast.3) | data formatting | bytes 3072

commit v2 on v0

--- a/solution.py
+++ b/solution.py
@@ -1,15 +1,289 @@
+import functools
 import math
 
 import jax
 import jax.numpy as jnp
 from jax import lax
+from jax.experimental import pallas as pl
+from jax.experimental.pallas import tpu as pltpu
 from jax.sharding import PartitionSpec as P
 
 BLOCK_WIDTH = 64
 COUNT_MAX = 4
+LANES = 128
+STEPS = (-1, 0, 1)
+OWNER_SHARE = 2
 
 
 damping = 0.5
+
+
+def split(value):
+    high = value.astype(jnp.bfloat16)
+    rest = value - high.astype(jnp.float32)
+    middle = rest.astype(jnp.bfloat16)
+    low = (rest - middle.astype(jnp.float32)).astype(jnp.bfloat16)
+    return high, middle, low
+
+
+def beside(*parts):
+    return jnp.concatenate(parts, axis=1)
+
+
+def above(*parts):
+    return jnp.concatenate(parts, axis=0)
+
+
+def wide_dot(left, right):
+    return jnp.dot(left, right, preferred_element_type=jnp.float32)
+
+
+def short_dot(left, right):
+    width = right.shape[1]
+    left_high, left_middle, _ = split(left)
+    right_high, right_middle, _ = split(right)
+    weights = above(
+        beside(right_high, right_middle), beside(right_high, jnp.zeros_like(right_middle))
+    )
+    both = wide_dot(beside(left_high, left_middle), weights)
+    return both[:, :width] + both[:, width:]
+
+
+def exact_dot(left, right):
+    width = right.shape[1]
+    left_high, left_middle, left_low = split(left)
+    right_high, right_middle, right_low = split(right)
+    line = beside(right_high, right_middle)
+    both = wide_dot(beside(left_high, left_middle), above(line, line))
+    small = wide_dot(beside(left_high, left_low), above(right_low, right_high))
+    return both[:, :width] + (both[:, width:] + small)
+
+
+def invert_modules(groups, example_total):
+    order = BLOCK_WIDTH
+    width = groups[0].shape[0]
+    row = lax.broadcasted_iota(jnp.int32, (width, width), 0)
+    column = lax.broadcasted_iota(jnp.int32, (width, width), 1)
+    same = row // order == column // order
+    diagonal = row == column
+    identity = jnp.where(diagonal, 1.0, 0.0)
+    lane = lax.broadcasted_iota(jnp.int32, (1, width), 1) // order
+    low, high = damping, order + damping
+    bound = (high + low) / (high - low)
+    scales, scaled, inverses, residuals = [], [], [], []
+    now, later = bound, 2.0 * bound * bound - 1.0
+    gain = 2.0 * now * now / later
+    for statistics in groups:
+        entries = jnp.sum(jnp.where(diagonal, statistics, 0.0), axis=0, keepdims=True)
+        traces = jnp.zeros((1, width), jnp.float32)
+        for module in range(width // order):
+            here = lane == module
+            total = jnp.sum(jnp.where(here, entries, 0.0), axis=1, keepdims=True)
+            traces = jnp.where(here, total, traces)
+        scale = order / traces
+        matrix = jnp.where(same, statistics * scale, 0.0) + damping * identity
+        residual = identity - (2.0 / (high + low)) * matrix
+        scales.append(scale)
+        scaled.append(matrix)
+        inverses.append((gain * 2.0 / (high + low)) * (identity + residual))
+        residuals.append(residual)
+    products = [short_dot(residual, residual) for residual in residuals]
+    residuals = [gain * product - (1.0 / later) * identity for product in products]
+    while later < 1e4:
+        now, later = later, 2.0 * later * later - 1.0
+        gain = 2.0 * now * now / later
+        products = [
+            short_dot(above(inverse, residual), residual)
+            for inverse, residual in zip(inverses, residuals)
+        ]
+        inverses = [
+            gain * (inverse + both[:width]) for inverse, both in zip(inverses, products)
+        ]
+        residuals = [gain * both[width:] - (1.0 / later) * identity for both in products]
+    errors = [
+        identity - exact_dot(matrix, inverse) for matrix, inverse in zip(scaled, inverses)
+    ]
+    products = [short_dot(inverse, error) for inverse, error in zip(inverses, errors)]
+    return [
+        (inverse + product) * (scale * example_total)
+        for inverse, product, scale in zip(inverses, products, scales)
+    ]
+
+
+def influence_tiles(rows, tiles_out, domain_count, shard_count, examples):
+    total, width = rows.shape
+    wide = domain_count * examples
+    statistics = lax.dot_general(
+        rows, rows, (((0,), (0,)), ((), ())), preferred_element_type=jnp.float32
+    )
+    spans = [slice(start, start + LANES) for start in range(0, width, LANES)]
+    inverses = invert_modules([statistics[span, span] for span in spans], float(total))
+    pieces = []
+    for span, inverse in zip(spans, inverses):
+        high, middle, low = split(inverse)
+        group = rows[:, span]
+        piece = wide_dot(beside(group, group), above(high, middle)) + wide_dot(group, low)
+        pieces.append(piece.astype(jnp.bfloat16))
+    products = lax.dot_general(
+        beside(*pieces), rows, (((1,), (1,)), ((), ())), preferred_element_type=jnp.float32
+    )
+    packed, taken = tiles_out.shape[1:]
+    slots = examples // packed
+    slot_width = taken // slots
+    slot = lax.broadcasted_iota(jnp.int32, (examples, taken), 1) // slot_width
+    for position in range(shard_count):
+        band = products[position * wide:(position + 1) * wide]
+        start = (position + STEPS[0]) * wide % total
+        band = pltpu.roll(band, (total - start) % total, 1)[:, :taken]
+        for number in range(domain_count):
+            tile = band[number * examples:(number + 1) * examples]
+            line = tile
+            for index in range(1, slots):
+                moved = pltpu.roll(tile, examples - index * packed, 0)
+                moved = pltpu.roll(moved, index * slot_width, 1)
+                line = jnp.where(slot == index, moved, line)
+            tiles_out[position * domain_count + number] = line[:packed]
+
+
+def kernel(domain_count, shard_count, owners, grads, pairs_in, out, own, pairs, rows_in,
+           tiles_out, tiles_in, load_sem, pairs_sem, send_sem, recv_sem, send_sem2, recv_sem2):
+    devices = domain_count * shard_count
+    domain, shard = lax.axis_index("domain"), lax.axis_index("shard")
+    here = shard * domain_count + domain
+    examples, full_width = own.shape
+    width = full_width // owners
+    owner = here < owners
+
+    def place(index):
+        return {"domain": index % domain_count, "shard": index // domain_count}
+
+    def rows_copy(source, target):
+        return pltpu.make_async_remote_copy(
+            src_ref=own.at[:, pl.ds(target * width, width)],
+            dst_ref=rows_in.at[source],
+            send_sem=send_sem.at[target],
+            recv_sem=recv_sem.at[source],
+            device_id=place(target),
+            device_id_type=pl.DeviceIdType.MESH,
+        )
+
+    def tile_copy(source, target):
+        return pltpu.make_async_remote_copy(
+            src_ref=tiles_out.at[target],
+            dst_ref=tiles_in.at[source],
+            send_sem=send_sem2.at[target],
+            recv_sem=recv_sem2.at[source],
+            device_id=place(target),
+            device_id_type=pl.DeviceIdType.MESH,
+        )
+
+    def for_others(count, act):
+        for index in range(count):
+            @pl.when(index != here)
+            def _():
+                act(index)
+
+    load = pltpu.make_async_copy(grads, own, load_sem)
+    load.start()
+    counts = pltpu.make_async_copy(pairs_in, pairs, pairs_sem)
+    counts.start()
+    barrier = pltpu.get_barrier_semaphore()
+
+    @pl.when(owner)
+    def _():
+        for_others(devices, lambda index: pl.semaphore_signal(
+            barrier, inc=1, device_id=place(index), device_id_type=pl.DeviceIdType.MESH
+        ))
+
+    load.wait()
+
+    @pl.when(owner)
+    def _():
+        mine = pl.ds(pl.multiple_of(here * width, LANES), width)
+        rows_in[pl.ds(here, 1)] = own[:, mine][None]
+        pl.semaphore_wait(barrier, owners - 1)
+
+    if owners < devices:
+        @pl.when(jnp.logical_not(owner))
+        def _():
+            pl.semaphore_wait(barrier, owners)
+
+    for_others(owners, lambda index: rows_copy(here, index).start())
+
+    @pl.when(owner)
+    def _():
+        for_others(devices, lambda index: rows_copy(index, 0).wait_recv())
+        total = devices * examples
+        rows = rows_in[...].astype(jnp.float32).reshape(total, width).astype(jnp.bfloat16)
+        influence_tiles(rows, tiles_out, domain_count, shard_count, examples)
+        for_others(devices, lambda index: tile_copy(here, index).start())
+        tiles_in[pl.ds(here, 1)] = tiles_out[pl.ds(here, 1)]
+
+    columns = out.shape[-1]
+    counts.wait()
+    column = lax.broadcasted_iota(jnp.int32, (examples, columns), 1)
+    column_domain = lax.rem(lax.div(column, examples), domain_count)
+    limits = jnp.zeros((examples, columns), jnp.int32)
+    for number in range(domain_count):
+        limit = pairs[domain, number] * (examples // COUNT_MAX)
+        limits = jnp.where(column_domain == number, limit, limits)
+    row = lax.broadcasted_iota(jnp.int32, (examples, columns), 0)
+    kept = (row < limits) & (lax.rem(column, examples) < limits)
+    for_others(owners, lambda index: tile_copy(index, 0).wait_recv())
+    packed, taken = tiles_in.shape[1:]
+    slots = examples // packed
+    slot_width = taken // slots
+    summed = jnp.sum(tiles_in[...], axis=0) * (1.0 / math.sqrt(full_width))
+    for index in range(slots):
+        part = slice(index * packed, (index + 1) * packed)
+        lines = summed[:, index * slot_width:index * slot_width + columns]
+        out[part, :] = jnp.where(kept[part], lines, 0.0)
+    for_others(owners, lambda index: rows_copy(here, index).wait_send())
+
+    @pl.when(owner)
+    def _():
+        for_others(devices, lambda index: tile_copy(here, index).wait_send())
+
+
+def owner_count(devices, full_width):
+    unit = math.lcm(LANES, BLOCK_WIDTH)
+    count = devices // OWNER_SHARE
+    return count if count and full_width % (count * unit) == 0 else 0
+
+
+def fused(gradients, pair_blocks):
+    domain_count, shard_count = lax.axis_size("domain"), lax.axis_size("shard")
+    devices = domain_count * shard_count
+    examples, full_width = gradients.shape[1:]
+    owners = owner_count(devices, full_width)
+    width = full_width // owners
+    columns = len(STEPS) * domain_count * examples
+    taken = pl.cdiv(columns, LANES) * LANES
+    slots = 2 if 2 * columns <= taken else 1
+    packed = examples // slots
+    one, per_owner, per_device = (
+        pltpu.SemaphoreType.DMA(shape) for shape in ((), (owners,), (devices,))
+    )
+    result = pl.pallas_call(
+        functools.partial(kernel, domain_count, shard_count, owners),
+        out_shape=jax.ShapeDtypeStruct((examples, columns), jnp.float32),
+        in_specs=[
+            pl.BlockSpec(memory_space=pl.ANY),
+            pl.BlockSpec(memory_space=pl.ANY),
+        ],
+        out_specs=pl.BlockSpec(memory_space=pltpu.VMEM),
+        scratch_shapes=[
+            pltpu.VMEM((examples, full_width), gradients.dtype),
+            pltpu.SMEM(pair_blocks.shape, pair_blocks.dtype),
+            pltpu.VMEM((devices, examples, width), gradients.dtype),
+            pltpu.VMEM((devices, packed, taken), jnp.float32),
+            pltpu.VMEM((owners, packed, taken), jnp.float32),
+            one, one, per_owner, per_device, per_device, per_owner,
+        ],
+        compiler_params=pltpu.CompilerParams(collective_id=0, has_side_effects=True),
+        name="influence",
+    )(gradients[0], pair_blocks)
+    return result[None]
 
 
 def shifted(value, axis, steps):
@@ -87,6 +361,16 @@
 
 def solution(mesh):
     placed = (P("domain", "shard", None), P())
+
+    def body(gradients, pair_blocks):
+        domain_count, shard_count = mesh.shape["domain"], mesh.shape["shard"]
+        devices = domain_count * shard_count
+        examples, full_width = gradients.shape[1:]
+        columns = len(STEPS) * domain_count * examples
+        if owner_count(devices, full_width) and examples % 8 == 0 and columns <= devices * examples:
+            return fused(gradients, pair_blocks)
+        return local(gradients, pair_blocks)
+
     return jax.shard_map(
-        local, mesh=mesh, in_specs=placed, out_specs=P("domain", "shard", None), check_vma=False
-    )
+        body, mesh=mesh, in_specs=placed, out_specs=P("domain", "shard", None), check_vma=False
+    )

time: 250 us -> 19.6 us (0.08)
  waiting for transfers between devices: 172 us -> 0 us
  other arithmetic: 48.3 us -> 0 us
  Pallas kernels: 0 us -> 18.2 us
  between operations: 13.2 us -> 0.01 us
  matrix products: 6.15 us -> 0 us
  starting transfers between devices: 5.21 us -> 0 us
    reduce_scatter x1 -> x0, waiting for transfers between devices: 84.3 us -> none  [local(): lax.psum_scatter(statistics, 'shard', scatter_dimension=0, tiled=True)]
    all_gather x1 -> x0, waiting for transfers between devices: 61.7 us -> none  [local(): lax.all_gather(invert(partial_sum, example_total), 'shard', axis=0, tiled...]
    another operation x7 -> x0, other arithmetic: 43.4 us -> none  [the longest x4 23.6 us: invert(): factor = jnp.linalg.cholesky(fisher)]
    pallas_call x0 -> x1, Pallas kernels: none -> 18.2 us  [fused(): pl.pallas_call(functools.partial(kernel, domain_count, shard_count, owner...]
    psum x1 -> x0, waiting for transfers between devices: 16.8 us -> none  [local(): partial_sum = lax.psum(partial_sum, 'domain')]
    ppermute x4 -> x0, waiting for transfers between devices: 9.43 us -> none  [shifted(): return lax.ppermute(value, axis, pairs)]
    dot_general x4 -> x0, matrix products: 5.74 us -> none  [the longest x1 2.7 us: local(): jnp.einsum('ibp,bpq->ibq', blocked.astype(jnp.float32), inverse, precisio...]
    ppermute x4 -> x0, starting transfers between devices: 5.12 us -> none  [shifted(): return lax.ppermute(value, axis, pairs)]
  transfers between devices with their start and end apart: 7 -> 0, of which waited for: 6 -> 0; matrix products, arithmetic and copies ran while one was open for 1% -> 0% of each run, Pallas kernels for 0% -> 0%
where the time goes in v2:
time: 19.6 us; the launch traced here: 19.5 us
  Pallas kernels  18.2 us (93%)
  local copies, waits for them, and re-layouts  1.28 us (7%)
    pallas_call x1, Pallas kernels, fused(): pl.pallas_call(functools.partial(kernel, domain_count, shard_count, owner...  18.2 us
    unnamed x1, local copies, waits for them, and re-layouts  1.28 us

profile of v2, /device:TPU:0, one launch (start us, length us, event | category | flops | bytes accessed | tf_op | source)
XLA Modules:
  0.0 19.5 jit_solution(6979172058899889858)
XLA Ops:
  0.0 18.2 %influence.1 = f32[8,48]{1,0:T(8,128)} custom-call(bf16[8,4096]{1,0:T(8,128)(2,1)} %bitcast.2, s32[2,2]{1,0:T(2,128)} %pairs_in.1), custom_call_target="tpu_custom_call" | custom-call | tf_op jit(solution)/shard_map/influence/pallas_call | solution.py:267
  18.2 1.3 %copy.4 = f32[1,8,48]{2,1,0:T(8,128)} copy(f32[1,8,48]{2,1,0:T(8,128)} %bitcast.3) | data formatting | bytes 3072

commit v3 on v2

--- a/solution.py
+++ b/solution.py
@@ -161,8 +161,8 @@
         return pltpu.make_async_remote_copy(
             src_ref=own.at[:, pl.ds(target * width, width)],
             dst_ref=rows_in.at[source],
-            send_sem=send_sem.at[target],
-            recv_sem=recv_sem.at[source],
+            send_sem=send_sem,
+            recv_sem=recv_sem,
             device_id=place(target),
             device_id_type=pl.DeviceIdType.MESH,
         )
@@ -171,8 +171,8 @@
         return pltpu.make_async_remote_copy(
             src_ref=tiles_out.at[target],
             dst_ref=tiles_in.at[source],
-            send_sem=send_sem2.at[target],
-            recv_sem=recv_sem2.at[source],
+            send_sem=send_sem2,
+            recv_sem=recv_sem2,
             device_id=place(target),
             device_id_type=pl.DeviceIdType.MESH,
         )
@@ -183,6 +183,20 @@
             def _():
                 act(index)
 
+    def wait_for(blocks, count, semaphore):
+        several = blocks.at[pl.ds(0, count)]
+        pltpu.make_async_copy(several, several, semaphore).wait()
+
+    def wait_for_owners(blocks, semaphore):
+        @pl.when(owner)
+        def _():
+            wait_for(blocks, owners - 1, semaphore)
+
+        if owners < devices:
+            @pl.when(jnp.logical_not(owner))
+            def _():
+                wait_for(blocks, owners, semaphore)
+
     load = pltpu.make_async_copy(grads, own, load_sem)
     load.start()
     counts = pltpu.make_async_copy(pairs_in, pairs, pairs_sem)
@@ -212,7 +226,7 @@
 
     @pl.when(owner)
     def _():
-        for_others(devices, lambda index: rows_copy(index, 0).wait_recv())
+        wait_for(rows_in, devices - 1, recv_sem)
         total = devices * examples
         rows = rows_in[...].astype(jnp.float32).reshape(total, width).astype(jnp.bfloat16)
         influence_tiles(rows, tiles_out, domain_count, shard_count, examples)
@@ -229,7 +243,8 @@
         limits = jnp.where(column_domain == number, limit, limits)
     row = lax.broadcasted_iota(jnp.int32, (examples, columns), 0)
     kept = (row < limits) & (lax.rem(column, examples) < limits)
-    for_others(owners, lambda index: tile_copy(index, 0).wait_recv())
+    wait_for_owners(rows_in, send_sem)
+    wait_for_owners(tiles_in, recv_sem2)
     packed, taken = tiles_in.shape[1:]
     slots = examples // packed
     slot_width = taken // slots
@@ -238,11 +253,10 @@
         part = slice(index * packed, (index + 1) * packed)
         lines = summed[:, index * slot_width:index * slot_width + columns]
         out[part, :] = jnp.where(kept[part], lines, 0.0)
-    for_others(owners, lambda index: rows_copy(here, index).wait_send())
 
     @pl.when(owner)
     def _():
-        for_others(devices, lambda index: tile_copy(here, index).wait_send())
+        wait_for(tiles_out, devices - 1, send_sem2)
 
 
 def owner_count(devices, full_width):
@@ -261,12 +275,9 @@
     taken = pl.cdiv(columns, LANES) * LANES
     slots = 2 if 2 * columns <= taken else 1
     packed = examples // slots
-    one, per_owner, per_device = (
-        pltpu.SemaphoreType.DMA(shape) for shape in ((), (owners,), (devices,))
-    )
     result = pl.pallas_call(
         functools.partial(kernel, domain_count, shard_count, owners),
-        out_shape=jax.ShapeDtypeStruct((examples, columns), jnp.float32),
+        out_shape=pltpu.VMEM((examples, columns), jnp.float32),
         in_specs=[
             pl.BlockSpec(memory_space=pl.ANY),
             pl.BlockSpec(memory_space=pl.ANY),
@@ -278,7 +289,7 @@
             pltpu.VMEM((devices, examples, width), gradients.dtype),
             pltpu.VMEM((devices, packed, taken), jnp.float32),
             pltpu.VMEM((owners, packed, taken), jnp.float32),
-            one, one, per_owner, per_device, per_device, per_owner,
+            *[pltpu.SemaphoreType.DMA] * 6,
         ],
         compiler_params=pltpu.CompilerParams(collective_id=0, has_side_effects=True),
         name="influence",

time: 19.6 us -> 17.4 us (0.89)
  Pallas kernels: 18.2 us -> 16.7 us
  local copies, waits for them, and re-layouts: 1.28 us -> 0.6 us
    pallas_call x1, Pallas kernels: 18.2 us -> 16.7 us  [fused(): pl.pallas_call(functools.partial(kernel, domain_count, shard_count, owner...]
    unnamed x1, local copies, waits for them, and re-layouts: 1.28 us -> 0.6 us
where the time goes in v3:
time: 17.4 us; the launch traced here: 17.3 us
  Pallas kernels  16.7 us (96%)
  local copies, waits for them, and re-layouts  0.6 us (3%)
    pallas_call x1, Pallas kernels, fused(): pl.pallas_call(functools.partial(kernel, domain_count, shard_count, owner...  16.7 us
    unnamed x1, local copies, waits for them, and re-layouts  0.6 us

profile of v3, /device:TPU:0, one launch (start us, length us, event | category | flops | bytes accessed | tf_op | source)
XLA Modules:
  0.0 17.3 jit_solution(6959902894225771088)
XLA Ops:
  0.0 16.7 %influence.1 = f32[8,48]{1,0:T(8,128)S(1)} custom-call(bf16[8,4096]{1,0:T(8,128)(2,1)} %bitcast.3, s32[2,2]{1,0:T(2,128)} %pairs_in.1), custom_call_target="tpu_custom_call" | custom-call | tf_op jit(solution)/shard_map/influence/pallas_call | solution.py:278
  16.7 0.6 %copy.4 = f32[1,8,48]{2,1,0:T(8,128)} copy(f32[1,8,48]{2,1,0:T(8,128)S(1)} %bitcast.2) | data formatting | bytes 3072

commit v4 on v3

--- a/solution.py
+++ b/solution.py
@@ -12,7 +12,7 @@
 COUNT_MAX = 4
 LANES = 128
 STEPS = (-1, 0, 1)
-OWNER_SHARE = 2
+OWNER_SHARE = 4
 
 
 damping = 0.5
@@ -38,14 +38,16 @@
     return jnp.dot(left, right, preferred_element_type=jnp.float32)
 
 
-def short_dot(left, right):
+def short_dot(lefts, right):
     width = right.shape[1]
-    left_high, left_middle, _ = split(left)
     right_high, right_middle, _ = split(right)
+    parts = [
+        (right_high, right_middle) if left is right else split(left)[:2] for left in lefts
+    ]
     weights = above(
         beside(right_high, right_middle), beside(right_high, jnp.zeros_like(right_middle))
     )
-    both = wide_dot(beside(left_high, left_middle), weights)
+    both = wide_dot(above(*[beside(*part) for part in parts]), weights)
     return both[:, :width] + both[:, width:]
 
 
@@ -87,30 +89,31 @@
         scaled.append(matrix)
         inverses.append((gain * 2.0 / (high + low)) * (identity + residual))
         residuals.append(residual)
-    products = [short_dot(residual, residual) for residual in residuals]
+    products = [short_dot([residual], residual) for residual in residuals]
     residuals = [gain * product - (1.0 / later) * identity for product in products]
     while later < 1e4:
         now, later = later, 2.0 * later * later - 1.0
         gain = 2.0 * now * now / later
         products = [
-            short_dot(above(inverse, residual), residual)
+            short_dot([inverse, residual] if later < 1e4 else [inverse], residual)
             for inverse, residual in zip(inverses, residuals)
         ]
         inverses = [
             gain * (inverse + both[:width]) for inverse, both in zip(inverses, products)
         ]
-        residuals = [gain * both[width:] - (1.0 / later) * identity for both in products]
+        if later < 1e4:
+            residuals = [gain * both[width:] - (1.0 / later) * identity for both in products]
     errors = [
         identity - exact_dot(matrix, inverse) for matrix, inverse in zip(scaled, inverses)
     ]
-    products = [short_dot(inverse, error) for inverse, error in zip(inverses, errors)]
+    products = [short_dot([inverse], error) for inverse, error in zip(inverses, errors)]
     return [
         (inverse + product) * (scale * example_total)
         for inverse, product, scale in zip(inverses, products, scales)
     ]
 
 
-def influence_tiles(rows, tiles_out, domain_count, shard_count, examples):
+def influence_tiles(rows, tiles_out, domain_count, shard_count, examples, send):
     total, width = rows.shape
     wide = domain_count * examples
     statistics = lax.dot_general(
@@ -143,42 +146,48 @@
                 moved = pltpu.roll(moved, index * slot_width, 1)
                 line = jnp.where(slot == index, moved, line)
             tiles_out[position * domain_count + number] = line[:packed]
-
-
-def kernel(domain_count, shard_count, owners, grads, pairs_in, out, own, pairs, rows_in,
+        if position in (0, shard_count - 1):
+            send(range(0 if position == 0 else domain_count, (position + 1) * domain_count))
+
+
+def kernel(domain_count, shard_count, owner_list, grads, pairs_in, out, own, pairs, rows_in,
            tiles_out, tiles_in, load_sem, pairs_sem, send_sem, recv_sem, send_sem2, recv_sem2):
     devices = domain_count * shard_count
     domain, shard = lax.axis_index("domain"), lax.axis_index("shard")
     here = shard * domain_count + domain
     examples, full_width = own.shape
+    owners = len(owner_list)
     width = full_width // owners
-    owner = here < owners
+    rank, owner = jnp.int32(0), jnp.bool_(False)
+    for index, device in enumerate(owner_list):
+        rank = jnp.where(here == device, index, rank)
+        owner = jnp.logical_or(owner, here == device)
 
     def place(index):
         return {"domain": index % domain_count, "shard": index // domain_count}
 
-    def rows_copy(source, target):
+    def rows_copy(target):
         return pltpu.make_async_remote_copy(
-            src_ref=own.at[:, pl.ds(target * width, width)],
-            dst_ref=rows_in.at[source],
+            src_ref=own.at[:, pl.ds(owner_list.index(target) * width, width)],
+            dst_ref=rows_in.at[here],
             send_sem=send_sem,
             recv_sem=recv_sem,
             device_id=place(target),
             device_id_type=pl.DeviceIdType.MESH,
         )
 
-    def tile_copy(source, target):
+    def tile_copy(target):
         return pltpu.make_async_remote_copy(
             src_ref=tiles_out.at[target],
-            dst_ref=tiles_in.at[source],
+            dst_ref=tiles_in.at[rank],
             send_sem=send_sem2,
             recv_sem=recv_sem2,
             device_id=place(target),
             device_id_type=pl.DeviceIdType.MESH,
         )
 
-    def for_others(count, act):
-        for index in range(count):
+    def for_others(devices_of, act):
+        for index in devices_of:
             @pl.when(index != here)
             def _():
                 act(index)
@@ -205,7 +214,7 @@
 
     @pl.when(owner)
     def _():
-        for_others(devices, lambda index: pl.semaphore_signal(
+        for_others(range(devices), lambda index: pl.semaphore_signal(
             barrier, inc=1, device_id=place(index), device_id_type=pl.DeviceIdType.MESH
         ))
 
@@ -213,7 +222,7 @@
 
     @pl.when(owner)
     def _():
-        mine = pl.ds(pl.multiple_of(here * width, LANES), width)
+        mine = pl.ds(pl.multiple_of(rank * width, LANES), width)
         rows_in[pl.ds(here, 1)] = own[:, mine][None]
         pl.semaphore_wait(barrier, owners - 1)
 
@@ -222,16 +231,19 @@
         def _():
             pl.semaphore_wait(barrier, owners)
 
-    for_others(owners, lambda index: rows_copy(here, index).start())
+    for_others(owner_list[::-1], lambda index: rows_copy(index).start())
 
     @pl.when(owner)
     def _():
         wait_for(rows_in, devices - 1, recv_sem)
         total = devices * examples
         rows = rows_in[...].astype(jnp.float32).reshape(total, width).astype(jnp.bfloat16)
-        influence_tiles(rows, tiles_out, domain_count, shard_count, examples)
-        for_others(devices, lambda index: tile_copy(here, index).start())
-        tiles_in[pl.ds(here, 1)] = tiles_out[pl.ds(here, 1)]
+
+        def send(targets):
+            for_others(targets, lambda index: tile_copy(index).start())
+
+        influence_tiles(rows, tiles_out, domain_count, shard_count, examples, send)
+        tiles_in[pl.ds(rank, 1)] = tiles_out[pl.ds(here, 1)]
 
     columns = out.shape[-1]
     counts.wait()
@@ -259,24 +271,33 @@
         wait_for(tiles_out, devices - 1, send_sem2)
 
 
-def owner_count(devices, full_width):
-    unit = math.lcm(LANES, BLOCK_WIDTH)
+def choose_owners(mesh, full_width):
+    domain_count, shard_count = mesh.shape["domain"], mesh.shape["shard"]
+    devices = domain_count * shard_count
     count = devices // OWNER_SHARE
-    return count if count and full_width % (count * unit) == 0 else 0
-
-
-def fused(gradients, pair_blocks):
+    if not count or full_width % (count * math.lcm(LANES, BLOCK_WIDTH)):
+        return []
+    flat = [mesh.devices[index % domain_count, index // domain_count] for index in range(devices)]
+    places = [getattr(device, "coords", None) or () for device in flat]
+
+    def hops(index):
+        return sum(abs(a - b) for a, b in zip(places[index], places[0]))
+
+    return sorted(range(devices), key=lambda index: (hops(index), index))[:count]
+
+
+def fused(gradients, pair_blocks, owner_list):
     domain_count, shard_count = lax.axis_size("domain"), lax.axis_size("shard")
     devices = domain_count * shard_count
     examples, full_width = gradients.shape[1:]
-    owners = owner_count(devices, full_width)
+    owners = len(owner_list)
     width = full_width // owners
     columns = len(STEPS) * domain_count * examples
     taken = pl.cdiv(columns, LANES) * LANES
     slots = 2 if 2 * columns <= taken else 1
     packed = examples // slots
     result = pl.pallas_call(
-        functools.partial(kernel, domain_count, shard_count, owners),
+        functools.partial(kernel, domain_count, shard_count, owner_list),
         out_shape=pltpu.VMEM((examples, columns), jnp.float32),
         in_specs=[
             pl.BlockSpec(memory_space=pl.ANY),
@@ -378,8 +399,9 @@
         devices = domain_count * shard_count
         examples, full_width = gradients.shape[1:]
         columns = len(STEPS) * domain_count * examples
-        if owner_count(devices, full_width) and examples % 8 == 0 and columns <= devices * examples:
-            return fused(gradients, pair_blocks)
+        owner_list = choose_owners(mesh, full_width)
+        if owner_list and examples % 8 == 0 and columns <= devices * examples:
+            return fused(gradients, pair_blocks, owner_list)
         return local(gradients, pair_blocks)
 
     return jax.shard_map(

time: 17.4 us -> 16.3 us (0.937)
  Pallas kernels: 16.7 us -> 15.5 us
    pallas_call x1, Pallas kernels: 16.7 us -> 15.5 us  [fused(): pl.pallas_call(functools.partial(kernel, domain_count, shard_count, owner...]
where the time goes in v4:
time: 16.3 us; the launch traced here: 16.1 us
  Pallas kernels  15.5 us (95%)
  local copies, waits for them, and re-layouts  0.6 us (4%)
    pallas_call x1, Pallas kernels, fused(): pl.pallas_call(functools.partial(kernel, domain_count, shard_count, owner...  15.5 us
    unnamed x1, local copies, waits for them, and re-layouts  0.6 us

profile of v4, /device:TPU:0, one launch (start us, length us, event | category | flops | bytes accessed | tf_op | source)
XLA Modules:
  0.0 16.1 jit_solution(10481544815802975182)
XLA Ops:
  0.0 15.5 %influence.1 = f32[8,48]{1,0:T(8,128)S(1)} custom-call(bf16[8,4096]{1,0:T(8,128)(2,1)} %bitcast.3, s32[2,2]{1,0:T(2,128)} %pairs_in.1), custom_call_target="tpu_custom_call" | custom-call | tf_op jit(solution)/shard_map/influence/pallas_call | solution.py:299
  15.5 0.6 %copy.4 = f32[1,8,48]{2,1,0:T(8,128)} copy(f32[1,8,48]{2,1,0:T(8,128)S(1)} %bitcast.2) | data formatting | bytes 3072

commit v5 on v4

--- a/solution.py
+++ b/solution.py
@@ -116,11 +116,15 @@
 def influence_tiles(rows, tiles_out, domain_count, shard_count, examples, send):
     total, width = rows.shape
     wide = domain_count * examples
-    statistics = lax.dot_general(
-        rows, rows, (((0,), (0,)), ((), ())), preferred_element_type=jnp.float32
-    )
     spans = [slice(start, start + LANES) for start in range(0, width, LANES)]
-    inverses = invert_modules([statistics[span, span] for span in spans], float(total))
+    statistics = [
+        lax.dot_general(
+            rows[:, span], rows[:, span], (((0,), (0,)), ((), ())),
+            preferred_element_type=jnp.float32,
+        )
+        for span in spans
+    ]
+    inverses = invert_modules(statistics, float(total))
     pieces = []
     for span, inverse in zip(spans, inverses):
         high, middle, low = split(inverse)

time: 16.3 us -> 16.3 us (level)
  no operation moved by 1% of the time
where the time goes in v5:
time: 16.3 us; the launch traced here: 16.1 us
  Pallas kernels  15.5 us (95%)
  local copies, waits for them, and re-layouts  0.6 us (4%)
    pallas_call x1, Pallas kernels, fused(): pl.pallas_call(functools.partial(kernel, domain_count, shard_count, owner...  15.5 us
    unnamed x1, local copies, waits for them, and re-layouts  0.6 us

profile of v5, /device:TPU:0, one launch (start us, length us, event | category | flops | bytes accessed | tf_op | source)
XLA Modules:
  0.0 16.1 jit_solution(12358124440288953253)
XLA Ops:
  0.0 15.5 %influence.1 = f32[8,48]{1,0:T(8,128)S(1)} custom-call(bf16[8,4096]{1,0:T(8,128)(2,1)} %bitcast.3, s32[2,2]{1,0:T(2,128)} %pairs_in.1), custom_call_target="tpu_custom_call" | custom-call | tf_op jit(solution)/shard_map/influence/pallas_call | solution.py:303
  15.5 0.6 %copy.4 = f32[1,8,48]{2,1,0:T(8,128)} copy(f32[1,8,48]{2,1,0:T(8,128)S(1)} %bitcast.2) | data formatting | bytes 3072
